TPU v7x, 256 devices: a whole 4x4x8 slice. The times are simulated.
256 devices in a mesh: seq: 64 (over y, z, core), ffn: 4 (over x).
Axes of the slice: x: 4, y: 4, z: 8, core: 2. Of those that a mesh axis runs over, the one named last changes fastest.
Arguments:
- child_feat: bfloat16 [32768, 1024], P('seq'), may hold values from -6 to 6
- parent_feat: bfloat16 [4096, 1024], P('seq'), may hold values from -6 to 6
- child_parent: int32 [32768], P('seq'), may hold values from 0 to 63
- owner: int32 [32768, 1], P('seq'), may hold values from 0 to 63; in each aligned block of 512 rows (0 to 511, 512 to 1023, ...) at most 16 rows name the same one
- log_gate: float32 [16, 65536], P('ffn', 'seq'), may hold values from -1 to 0
- norm_gain: bfloat16 [1024], replicated, may hold values from 0.3984375 to 1.59375
- w_query: bfloat16 [1024, 1024], P(None, 'ffn'), may hold values from -0.1875 to 0.1875
- w_key: bfloat16 [1024, 1024], P(None, 'ffn'), may hold values from -0.1875 to 0.1875
- w_value: bfloat16 [1024, 1024], P(None, 'ffn'), may hold values from -0.1875 to 0.1875
- head_gain: bfloat16 [1024], P('ffn'), may hold values from 0.25 to 1.75
- w_out: bfloat16 [1024, 1024], P('ffn'), may hold values from -0.1875 to 0.1875
- ffn_gain: bfloat16 [1024], replicated, may hold values from 0.3984375 to 1.59375
- w_up: bfloat16 [1024, 4096], P(None, 'ffn'), may hold values from -0.1875 to 0.1875
- w_down: bfloat16 [4096, 1024], P('ffn'), may hold values from -0.09375 to 0.09375
Outputs:
- child_out: bfloat16 [32768, 1024], P('seq', 'ffn')
Inputs may be any that keep to these rules, and one draw needn't show every extreme that they name: The parent of child i is row (i // 512) * 64 + child_parent[i] of parent_feat. Among the 512 children of one index of seq, at most 16 name the same owner, and in every draw some owner is named exactly 16 times by some block.
All inputs are finite; a program needn't handle non-finite values.
Results may differ from a plain program's by a relative error of at most 0.013.
Values may be sent and summed in bfloat16 or wider, within the bound.
A program may use at most 64 MiB of HBM per device.

v0:
```python
import jax
import jax.numpy as jnp
from jax import lax
from jax.sharding import Mesh
from jax.sharding import PartitionSpec as P

D = 1024
HD = 64
PAR_DEV = 64
SLOT_DEV = 1024
SEQ = ("seq_0", "seq_1", "seq_2")


EPSILON = 1e-05
PRECISE = lax.Precision.HIGHEST


def in_order(blocks, dim):
    lengths = list(blocks.shape[1:])
    lengths[dim] *= blocks.shape[0]
    return jnp.moveaxis(blocks, 0, dim).reshape(lengths)


def copy_for_each(array, axis):
    copies = jnp.broadcast_to(array, (lax.axis_size(axis), *array.shape))
    return lax.all_to_all(copies, axis, split_axis=0, concat_axis=0, tiled=True)


def gathered_copies(array, axis, dim):
    return in_order(copy_for_each(array, axis), dim)


def nothing_yet(array, identity):
    return jax.tree.map(
        lambda a, e: jnp.broadcast_to(jnp.asarray(e, a.dtype), a.shape), array, identity
    )


def carried_in(array, axes, combine, identity):
    before = start = nothing_yet(array, identity)
    so_far = array
    for axis in reversed(axes):
        peers, mine = (lax.axis_size(axis), lax.axis_index(axis))
        pieces = jax.tree.map(
            lambda part, kind: lax.all_gather(part.astype(kind), axis),
            so_far,
            (jnp.bfloat16, jnp.bfloat16),
        )
        inside, so_far = (start, start)
        for k in range(peers):
            passed = k < mine
            so_far = combine(
                so_far, jax.tree.map(lambda part, own: part[k].astype(own.dtype), pieces, array)
            )
            inside = jax.tree.map(lambda new, old: jnp.where(passed, new, old), so_far, inside)
        before = combine(inside, before)
    return before


def cut_along(array, dim, peers):
    lengths = array.shape
    blocks = array.reshape(*lengths[:dim], peers, lengths[dim] // peers, *lengths[dim + 1 :])
    return jnp.moveaxis(blocks, dim, 0)


def sum_at_owner(array, axis, dim):
    blocks = cut_along(array, dim, lax.axis_size(axis))
    arrived = lax.all_to_all(blocks, axis, split_axis=0, concat_axis=0, tiled=True)
    return arrived.astype(jnp.float32).sum(axis=0)


def over_copies(array, axis):
    return copy_for_each(array, axis).sum(axis=0)


def row_norm(values, scales):
    return values * lax.rsqrt(jnp.mean(values * values, axis=-1, keepdims=True) + EPSILON) * scales


def on_device(
    child_feat,
    parent_feat,
    child_parent,
    owner,
    log_gate,
    norm_gain,
    w_query,
    w_key,
    w_value,
    head_gain,
    w_out,
    ffn_gain,
    w_up,
    w_down,
):
    seq_count = lax.axis_size(SEQ)
    ffn_count = lax.axis_size("ffn")
    capacity = SLOT_DEV // seq_count
    column_share = D // ffn_count
    ffn_index = lax.axis_index("ffn")
    local_heads = log_gate.shape[0]
    parent_pick = (child_parent[:, None] == jnp.arange(PAR_DEV, dtype=jnp.int32)[None, :]).astype(
        jnp.bfloat16
    )
    joined = (
        child_feat.astype(jnp.float32)
        + jnp.dot(parent_pick, parent_feat, preferred_element_type=jnp.float32)
    ).astype(jnp.bfloat16)
    owner_ids = owner[:, 0]
    matched = (owner_ids[:, None] == jnp.arange(seq_count, dtype=jnp.int32)[None, :]).astype(
        jnp.int32
    )
    within = jnp.sum(matched * (jnp.cumsum(matched, axis=0) - 1), axis=1)
    target = owner_ids * capacity + within
    quarter_cols = lax.dynamic_slice_in_dim(joined, ffn_index * column_share, column_share, 1)
    outgoing = jnp.zeros((SLOT_DEV, column_share), jnp.bfloat16).at[target].set(quarter_cols)
    arrived = lax.all_to_all(
        outgoing.reshape(seq_count, capacity, column_share),
        SEQ,
        split_axis=0,
        concat_axis=0,
        tiled=True,
    )
    slot_rows = gathered_copies(arrived.reshape(SLOT_DEV, column_share), "ffn", 1)
    residual_in = slot_rows.astype(jnp.float32)
    normed = row_norm(residual_in, norm_gain.astype(jnp.float32)).astype(jnp.bfloat16)
    queries = (
        jnp.dot(normed, w_query, preferred_element_type=jnp.float32)
        .astype(jnp.bfloat16)
        .reshape(SLOT_DEV, local_heads, HD)
    )
    key_rows = (
        jnp.dot(normed, w_key, preferred_element_type=jnp.float32)
        .astype(jnp.bfloat16)
        .reshape(SLOT_DEV, local_heads, HD)
    )
    value_rows = (
        jnp.dot(normed, w_value, preferred_element_type=jnp.float32)
        .astype(jnp.bfloat16)
        .reshape(SLOT_DEV, local_heads, HD)
    )
    running = jnp.cumsum(log_gate, axis=1)
    position = jnp.arange(SLOT_DEV, dtype=jnp.int32)
    causal = (position[:, None] >= position[None, :])[None]
    spacing = running[:, :, None] - running[:, None, :]
    decay_mat = jnp.where(causal, jnp.exp(jnp.where(causal, spacing, 0.0)), 0.0)
    scores = jnp.einsum("shd,thd->hst", queries, key_rows, preferred_element_type=jnp.float32)
    mixing = (scores * decay_mat).astype(jnp.bfloat16)
    inside = jnp.einsum("hst,thd->shd", mixing, value_rows, preferred_element_type=jnp.float32)
    block_end = running[:, -1]
    fading = jnp.exp(block_end[:, None] - running).T
    local_state = jnp.einsum(
        "shd,she->hde",
        key_rows.astype(jnp.float32) * fading[:, :, None],
        value_rows.astype(jnp.float32),
        precision=PRECISE,
    )
    empty_state = jnp.zeros((local_heads, HD, HD), jnp.float32)

    def compose(earlier, latter):
        return (earlier[0] * latter[0], latter[0][:, None, None] * earlier[1] + latter[1])

    prefix = carried_in(
        (jnp.exp(block_end), local_state),
        SEQ,
        compose,
        (jnp.ones((local_heads,), jnp.float32), empty_state),
    )
    incoming = prefix[1]
    outside = jnp.exp(running).T[:, :, None] * jnp.einsum(
        "shd,hde->she", queries.astype(jnp.float32), incoming, precision=PRECISE
    )
    combined = inside + outside
    head_scales = head_gain.astype(jnp.float32).reshape(local_heads, HD)
    per_head = (
        combined
        * lax.rsqrt(jnp.mean(combined * combined, axis=-1, keepdims=True) + EPSILON)
        * head_scales[None]
    )
    flattened = per_head.astype(jnp.bfloat16).reshape(SLOT_DEV, local_heads * HD)
    projected = jnp.dot(flattened, w_out, preferred_element_type=jnp.float32)
    mixed_part = sum_at_owner(projected.astype(jnp.bfloat16), "ffn", 1)
    kept_cols = (
        lax.dynamic_slice_in_dim(residual_in, ffn_index * column_share, column_share, 1)
        + mixed_part
    )
    squares = over_copies(jnp.sum(kept_cols * kept_cols, axis=1), "ffn")
    gain_part = lax.dynamic_slice_in_dim(
        ffn_gain, ffn_index * column_share, column_share, 0
    ).astype(jnp.float32)
    normed_part = (kept_cols * lax.rsqrt(squares / D + EPSILON)[:, None] * gain_part).astype(
        jnp.bfloat16
    )
    second = gathered_copies(normed_part, "ffn", 1)
    expanded = jax.nn.gelu(jnp.dot(second, w_up, preferred_element_type=jnp.float32)).astype(
        jnp.bfloat16
    )
    ffn_part = sum_at_owner(
        jnp.dot(expanded, w_down, preferred_element_type=jnp.float32).astype(jnp.bfloat16), "ffn", 1
    )
    refined = (kept_cols + ffn_part).astype(jnp.bfloat16)
    returned = lax.all_to_all(
        refined.reshape(seq_count, capacity, column_share),
        SEQ,
        split_axis=0,
        concat_axis=0,
        tiled=True,
    )
    return returned.reshape(SLOT_DEV, column_share)[target]


def solution(mesh):
    split = Mesh(
        mesh.devices.reshape(4, 8, 2, mesh.shape["ffn"]), ("seq_0", "seq_1", "seq_2", "ffn")
    )
    in_specs = (
        P(SEQ, None),
        P(SEQ, None),
        P(SEQ),
        P(SEQ, None),
        P("ffn", SEQ),
        P(),
        P(None, "ffn"),
        P(None, "ffn"),
        P(None, "ffn"),
        P("ffn"),
        P("ffn", None),
        P(),
        P(None, "ffn"),
        P("ffn", None),
    )
    out_specs = P(SEQ, "ffn")
    return jax.shard_map(
        on_device, mesh=split, in_specs=in_specs, out_specs=out_specs, check_vma=False
    )
```

profile of v0, /device:TPU:2, one launch (start us, length us, event | category | flops | bytes accessed | tf_op | source)
XLA Modules:
  0.0 252.3 jit_solution(9374303752773200157)
XLA Ops:
  0.0 0.8 fusion.93
  0.8 1.2 reduce-window.14
  2.1 0.2 slice_reduce_fusion
  2.3 0.8 fusion.70
  3.1 0.7 compare_select_fusion
  3.8 2.8 %fusion.29 = f32[512,1024]{1,0:T(8,128)} fusion(bf16[64,1024]{1,0:T(8,128)(2,1)} %param.15, s32[512]{0:T(512)} %param.16), kind=kOutput, calls=%fused_computation.48 | convolution fusion | flops 67141632 | bytes 2230272 | tf_op jit(solution)/shard_map/dot_general | solution.py:107
  6.6 3.7 %scatter_custom_fusion = bf16[1024,256]{1,0:T(8,128)(2,1)} fusion(s32[512]{0:T(512)S(1)} %bitcast.337, f32[512,1024]{1,0:T(8,128)} %fusion.29, s32[]{:T(128)} %constant.28.clone.1, s32[]{:T(128)S(6)} %select_n.212, bf16[512,1024]{1,0:T(8,128)(2,1)} %param.14, bf16[]{:T(256)} %constant.26.clone.1), kind=kCustom, calls=%fused_computation.44 | custom fusion | flops 393216 | bytes 1311748 | tf_op jit(solution)/shard_map/scatter | solution.py:116
  10.3 12.1 %all-to-all-start = ((bf16[64,16,256]{2,1,0:T(8,128)(2,1)}), bf16[64,16,256]{2,1,0:T(8,128)(2,1)S(1)}, u32[]{:S(2)}, u32[]{:S(2)}) async-start(bf16[64,16,256]{2,1,0:T(8,128)(2,1)} %bitcast.5), calls=%async_computation | async-start | bytes 1048576 | tf_op jit(solution)/shard_map/all_to_all | solution.py:117
  22.4 1.1 reduce-window.16
  24.2 0.6 dynamic-slice
  25.5 0.2 dynamic-update-slice
  25.7 2.4 all-reduce
  28.2 18.0 %all-gather.2 = bf16[8,1,4]{2,1,0:T(2,128)(2,1)S(1)} all-gather(bf16[1,1,4]{2,1,0:T(2,128)(2,1)S(1)} %get-tuple-element.24), channel_id=1, replica_groups=mesh['seq_0'=4,'seq_1'=8,'seq_2'=2,'ffn'=4] {'seq_1'}, dimensions={0}, use_global_device_ids=true | all-gather | bytes 72 | tf_op jit(solution)/shard_map/all_gather | solution.py:45
  46.4 1.6 broadcast_in_dim.33
  48.1 5.1 %all-to-all-start.1 = ((bf16[4,1024,256]{1,2,0:T(8,128)(2,1)}), bf16[4,1024,256]{1,2,0:T(8,128)(2,1)}, u32[]{:S(2)}, u32[]{:S(2)}) async-start(bf16[4,1024,256]{1,2,0:T(8,128)(2,1)} %broadcast_in_dim.33), calls=%async_computation.1 | async-start | bytes 4194304 | tf_op jit(solution)/shard_map/all_to_all | solution.py:26
  53.1 1.3 iota_compare_fusion
  54.4 9.8 %all-gather.3 = bf16[4,1,4]{2,1,0:T(2,128)(2,1)S(1)} all-gather(bf16[1,1,4]{2,1,0:T(2,128)(2,1)S(1)} %fusion.142), channel_id=1, replica_groups=mesh['seq_0'=4,'seq_1'=8,'seq_2'=2,'ffn'=4] {'seq_0'}, dimensions={0}, use_global_device_ids=true | all-gather | bytes 40 | tf_op jit(solution)/shard_map/all_gather | solution.py:45
  64.6 10.9 %all-to-all-done.1 = bf16[4,1024,256]{1,2,0:T(8,128)(2,1)} async-done(((bf16[4,1024,256]{1,2,0:T(8,128)(2,1)}), bf16[4,1024,256]{1,2,0:T(8,128)(2,1)}, u32[]{:S(2)}, u32[]{:S(2)}) %all-to-all-start.1) | async-done | bytes 2097184 | tf_op jit(solution)/shard_map/all_to_all | solution.py:26
  75.5 2.1 multiply_reduce_fusion
  77.6 4.1 %multiply_convert_fusion.1 = (bf16[1024,1024]{0,1:T(8,128)(2,1)S(1)}, f32[4,1024,256]{1,2,0:T(8,128)}) fusion(f32[1024]{0:T(1024)S(1)} %convert_element_type.433, f32[1024]{0:T(1024)S(1)} %add_rsqrt_fusion.2, bf16[4,1024,256]{1,2,0:T(8,128)(2,1)} %all-to-all-done.1), kind=kLoop, calls=%fused_computation.15 | loop fusion | flops 4194304 | bytes 8396800 | tf_op jit(solution)/shard_map/convert_element_type | solution.py:126
  81.8 0.8 convolution_convert_fusion.3
  82.5 0.3 copy-done.6
  82.8 1.6 convolution_convert_fusion.2
  84.4 0.8 convolution_convert_fusion.1
  85.1 0.7 convolution_convert_fusion.4
  85.8 1.9 all-gather.1
  87.8 25.6 %all_gather.31 = bf16[8,4,64,64]{3,2,1,0:T(8,128)(2,1)S(1)} all-gather(bf16[1,4,64,64]{3,2,1,0:T(8,128)(2,1)S(1)} %fusion.68), channel_id=1, replica_groups=mesh['seq_0'=4,'seq_1'=8,'seq_2'=2,'ffn'=4] {'seq_1'}, dimensions={0}, use_global_device_ids=true | all-gather | bytes 294912 | tf_op jit(solution)/shard_map/all_gather | solution.py:45
  113.6 12.6 %all_gather.32 = bf16[4,4,64,64]{3,2,1,0:T(8,128)(2,1)S(1)} all-gather(bf16[1,4,64,64]{3,2,1,0:T(8,128)(2,1)S(1)} %fusion.92), channel_id=1, replica_groups=mesh['seq_0'=4,'seq_1'=8,'seq_2'=2,'ffn'=4] {'seq_0'}, dimensions={0}, use_global_device_ids=true | all-gather | bytes 163840 | tf_op jit(solution)/shard_map/all_gather | solution.py:45
  126.2 9.6 %fusion.18 = f32[1024,4,64]{0,2,1:T(8,128)} fusion(bf16[1024,4,64]{0,2,1:T(8,128)(2,1)} %bitcast.344, bf16[1024,4,64]{0,2,1:T(8,128)(2,1)} %bitcast.341, bf16[1024,4,64]{0,2,1:T(8,128)(2,1)} %bitcast.346, f32[4,1024]{1,0:T(4,128)S(1)} %bitcast.332, pred[1024,1024]{1,0:T(8,128)(4,1)} %iota_compare_fusion), kind=kOutput, calls=%fused_computation.25 | convolution fusion | flops 1094713344 | bytes 3686400 | tf_op jit(solution)/shard_map/hst,thd->shd/dot_general | solution.py:149
  135.7 2.5 multiply_reduce_fusion.2
  138.4 0.8 convolution_convert_fusion
  139.1 21.3 %all_to_all.36 = bf16[4,1024,256]{1,2,0:T(8,128)(2,1)S(1)} all-to-all(bf16[4,1024,256]{1,2,0:T(8,128)(2,1)S(1)} %bitcast.324), channel_id=1, replica_groups=mesh['seq_0'=4,'seq_1'=8,'seq_2'=2,'ffn'=4] {'ffn'}, dimensions={0} | all-to-all | bytes 4194304 | tf_op jit(solution)/shard_map/all_to_all | solution.py:68
  160.5 0.4 convert_reduce_fusion.1
  160.9 1.4 multiply_reduce_fusion.1
  162.3 0.6 broadcast_in_dim.39
  162.9 4.7 %all-to-all-start.3 = ((f32[4,1,1024]{2,1,0:T(1,128)}), f32[4,1,1024]{2,1,0:T(1,128)S(1)}, u32[]{:S(2)}, u32[]{:S(2)}) async-start(f32[4,1,1024]{2,1,0:T(1,128)} %broadcast_in_dim.39), calls=%async_computation.3 | async-start | bytes 32768 | tf_op jit(solution)/shard_map/all_to_all | solution.py:26
  167.6 0.8 dynamic-slice_convert_fusion
  168.3 3.3 %all-to-all-done.3 = f32[4,1,1024]{2,1,0:T(1,128)S(1)} async-done(((f32[4,1,1024]{2,1,0:T(1,128)}), f32[4,1,1024]{2,1,0:T(1,128)S(1)}, u32[]{:S(2)}, u32[]{:S(2)}) %all-to-all-start.3) | async-done | bytes 16416 | tf_op jit(solution)/shard_map/all_to_all | solution.py:26
  171.8 0.3 broadcast_in_dim.40
  172.1 19.7 %all_to_all.37 = bf16[4,1024,256]{1,2,0:T(8,128)(2,1)} all-to-all(bf16[4,1024,256]{1,2,0:T(8,128)(2,1)S(1)} %broadcast_in_dim.40), channel_id=1, replica_groups=mesh['seq_0'=4,'seq_1'=8,'seq_2'=2,'ffn'=4] {'ffn'}, dimensions={0} | all-to-all | bytes 4194304 | tf_op jit(solution)/shard_map/all_to_all | solution.py:26
  191.8 8.9 %fusion.15 = bf16[1024,1024]{0,1:T(8,128)(2,1)} fusion(bf16[1024,1024]{1,0:T(8,128)(2,1)S(1)} %copy-done, bf16[1024,1024]{0,1:T(8,128)(2,1)} %bitcast.326, bf16[1024,1024]{1,0:T(8,128)(2,1)} %param.26), kind=kOutput, calls=%fused_computation.23 | convolution fusion | flops 4305453056 | bytes 8388608 | tf_op jit(solution)/shard_map/dot_general | solution.py:199
  200.7 20.1 %all_to_all.38 = bf16[4,1024,256]{1,2,0:T(8,128)(2,1)S(1)} all-to-all(bf16[4,1024,256]{1,2,0:T(8,128)(2,1)} %bitcast.327), channel_id=1, replica_groups=mesh['seq_0'=4,'seq_1'=8,'seq_2'=2,'ffn'=4] {'ffn'}, dimensions={0} | all-to-all | bytes 4194304 | tf_op jit(solution)/shard_map/all_to_all | solution.py:68
  220.8 0.4 convert_reduce_fusion
  221.2 0.9 add_convert_fusion
  222.1 2.1 copy.41
  224.2 8.3 %all-to-all-start.6 = ((bf16[64,16,256]{2,1,0:T(8,128)(2,1)}), bf16[64,16,256]{2,1,0:T(8,128)(2,1)S(1)}, u32[]{:S(2)}, u32[]{:S(2)}) async-start(bf16[64,16,256]{2,1,0:T(8,128)(2,1)} %bitcast.61), calls=%async_computation.6 | async-start | bytes 1048576 | tf_op jit(solution)/shard_map/all_to_all | solution.py:202
  232.5 17.2 %all-to-all-done.6 = bf16[64,16,256]{2,1,0:T(8,128)(2,1)S(1)} async-done(((bf16[64,16,256]{2,1,0:T(8,128)(2,1)}), bf16[64,16,256]{2,1,0:T(8,128)(2,1)S(1)}, u32[]{:S(2)}, u32[]{:S(2)}) %all-to-all-start.6) | async-done | bytes 524320 | tf_op jit(solution)/shard_map/all_to_all | solution.py:202
  249.7 2.6 %gather_fusion = bf16[512,256]{1,0:T(8,128)(2,1)} fusion(bf16[1024,256]{1,0:T(8,128)(2,1)S(1)} %bitcast.323, s32[1024]{0:T(1024)S(1)} %pad_clamp_fusion), kind=kCustom, calls=%fused_computation | custom fusion | bytes 526336 | tf_op jit(solution)/shard_map/gather | solution.py:209
  (54 shorter events, 1.9 us)
Async XLA Ops:
  0.0 191.8 %copy-start = (bf16[1024,1024]{1,0:T(8,128)(2,1)S(1)}, bf16[1024,1024]{1,0:T(8,128)(2,1)}, u32[]{:S(2)}) copy-start(bf16[1024,1024]{1,0:T(8,128)(2,1)} %param.27) | copy-start | bytes 6291460
  3.8 18.6 %copy-start.2 = (f32[4,1024]{1,0:T(4,128)S(1)}, f32[4,1024]{1,0:T(4,128)}, u32[]{:S(2)}) copy-start(f32[4,1024]{1,0:T(4,128)} %param.18) | copy-start | bytes 49156
  3.8 20.4 %copy-start.10 = (u32[256]{0:T(256)S(1)}, u32[256]{0:T(256)}, u32[]{:S(2)}) copy-start(u32[256]{0:T(256)} %constant.79) | copy-start | bytes 3076
  10.3 35.9 %all-to-all-start = ((bf16[64,16,256]{2,1,0:T(8,128)(2,1)}), bf16[64,16,256]{2,1,0:T(8,128)(2,1)S(1)}, u32[]{:S(2)}, u32[]{:S(2)}) async-start(bf16[64,16,256]{2,1,0:T(8,128)(2,1)} %bitcast.5), calls=%async_computation | async-start | bytes 1048576 | tf_op jit(solution)/shard_map/all_to_all | solution.py:117
  48.1 16.2 %copy-start.3 = (bf16[1024]{0:T(1024)(128)(2,1)S(1)}, bf16[1024]{0:T(1024)(128)(2,1)}, u32[]{:S(2)}) copy-start(bf16[1024]{0:T(1024)(128)(2,1)} %param.19) | copy-start | bytes 6148
  48.1 16.2 %copy-start.4 = (bf16[256]{0:T(256)(128)(2,1)S(1)}, bf16[256]{0:T(256)(128)(2,1)}, u32[]{:S(2)}) copy-start(bf16[256]{0:T(256)(128)(2,1)} %param.23) | copy-start | bytes 1540
  48.1 27.5 %all-to-all-start.1 = ((bf16[4,1024,256]{1,2,0:T(8,128)(2,1)}), bf16[4,1024,256]{1,2,0:T(8,128)(2,1)}, u32[]{:S(2)}, u32[]{:S(2)}) async-start(bf16[4,1024,256]{1,2,0:T(8,128)(2,1)} %broadcast_in_dim.33), calls=%async_computation.1 | async-start | bytes 4194304 | tf_op jit(solution)/shard_map/all_to_all | solution.py:26
  77.6 4.1 %copy-start.5 = (bf16[1024,256]{1,0:T(8,128)(2,1)S(1)}, bf16[1024,256]{1,0:T(8,128)(2,1)}, u32[]{:S(2)}) copy-start(bf16[1024,256]{1,0:T(8,128)(2,1)} %param.22) | copy-start | bytes 1572868
  81.7 1.0 copy-start.6
  82.8 2.3 copy-start.8
  82.8 1.6 copy-start.7
  85.1 41.0 %copy-start.9 = (bf16[1024,256]{0,1:T(8,128)(2,1)}, bf16[1024,256]{0,1:T(8,128)(2,1)S(1)}, u32[]{:S(2)}) copy-start(bf16[1024,256]{0,1:T(8,128)(2,1)S(1)} %convolution_convert_fusion.1) | copy-start | bytes 1572868
  135.7 2.6 %copy-start.1 = (bf16[256,1024]{1,0:T(8,128)(2,1)S(1)}, bf16[256,1024]{1,0:T(8,128)(2,1)}, u32[]{:S(2)}) copy-start(bf16[256,1024]{1,0:T(8,128)(2,1)} %param.24) | copy-start | bytes 1572868
  162.9 8.7 %all-to-all-start.3 = ((f32[4,1,1024]{2,1,0:T(1,128)}), f32[4,1,1024]{2,1,0:T(1,128)S(1)}, u32[]{:S(2)}, u32[]{:S(2)}) async-start(f32[4,1,1024]{2,1,0:T(1,128)} %broadcast_in_dim.39), calls=%async_computation.3 | async-start | bytes 32768 | tf_op jit(solution)/shard_map/all_to_all | solution.py:26
  224.2 25.5 %all-to-all-start.6 = ((bf16[64,16,256]{2,1,0:T(8,128)(2,1)}), bf16[64,16,256]{2,1,0:T(8,128)(2,1)S(1)}, u32[]{:S(2)}, u32[]{:S(2)}) async-start(bf16[64,16,256]{2,1,0:T(8,128)(2,1)} %bitcast.61), calls=%async_computation.6 | async-start | bytes 1048576 | tf_op jit(solution)/shard_map/all_to_all | solution.py:202
where the time goes:
time: 255 us; the launch traced here: 252 us
  blocking collectives  131 us (51%)
  waiting for transfers between devices  31.4 us (12%)
  starting transfers between devices  30.2 us (12%)
  matrix products  28.2 us (11%)
  other arithmetic  21 us (8%)
  local copies, waits for them, and re-layouts  9.13 us (4%)
    all_gather x5, blocking collectives, carried_in(): lax.all_gather(part.astype(kind), axis)  67.9 us
    all_to_all x2, blocking collectives, sum_at_owner(): lax.all_to_all(blocks, axis, split_axis=0, concat_axis=0, tiled=True)  41.4 us
    all_to_all x1, blocking collectives, copy_for_each(): return lax.all_to_all(copies, axis, split_axis=0, concat_axis=0, tiled=True)  19.7 us
    all_to_all x1, waiting for transfers between devices, on_device(): lax.all_to_all(refined.reshape(seq_count, capacity, column_share), SEQ, s...  17.2 us
    all_to_all x2, waiting for transfers between devices, copy_for_each(): return lax.all_to_all(copies, axis, split_axis=0, concat_axis=0, tiled=True)  14.2 us
    all_to_all x1, starting transfers between devices, on_device(): lax.all_to_all(outgoing.reshape(seq_count, capacity, column_share), SEQ,...  12.1 us
    all_to_all x2, starting transfers between devices, copy_for_each(): return lax.all_to_all(copies, axis, split_axis=0, concat_axis=0, tiled=True)  9.75 us
    dot_general x1, matrix products, on_device(): jnp.einsum('hst,thd->shd', mixing, value_rows, preferred_element_type=jnp...  9.56 us
  transfers between devices with their start and end apart: 4, of which 3 were waited for; matrix products, arithmetic and copies ran while one was open for 2% of the time, Pallas kernels for 0%

commit v1 on v0

v1 whole, which is shorter than its diff:
```python
import jax
import jax.numpy as jnp
from jax import lax
from jax.experimental import pallas as pl
from jax.experimental.pallas import tpu as pltpu
from jax.sharding import PartitionSpec as P

D = 1024
HD = 64
HEADS = 4
Q = 256
TOK = 512
PAR = 64
SLOT = 1024
N = 64
CAP = 16
GRP = 16
CH = 256
ROWS = 128
HALF = 64
EPS = 1e-05
F32 = jnp.float32
BF16 = jnp.bfloat16
MESH = pl.DeviceIdType.MESH
EXACT = lax.Precision.HIGHEST
REL = (0, 1, 3, 2)


def nt(a, b, precision=None):
    return lax.dot_general(
        a, b, (((1,), (1,)), ((), ())), precision=precision, preferred_element_type=F32
    )


def tn(a, b):
    return lax.dot_general(a, b, (((0,), (0,)), ((), ())), preferred_element_type=F32)


def nn(a, b, precision=None):
    return jnp.dot(a, b, precision=precision, preferred_element_type=F32)


def iota(shape, dim):
    return lax.broadcasted_iota(jnp.int32, shape, dim)


def kernel(
    child, parent, cp_row, own_row, gate, ngain, wq, wk, wv, hgain, wo, fgain, wu, wd,
    out,
    child_v, parent_v, wqkv, wo_v, wu_v, wd_v,
    joined, pick_t, outgoing, slots, normed, qkv, att, ccol, crow, loc, offs,
    s_send, s_recv, p_send, p_recv, heads_out, back,
    part, via, comb, fin, hid, hb,
    in_sem, a_send, a_recv, g_send, g_recv, st_send, st_recv, pf_send, pf_recv, b_send, b_recv,
    v_send, v_recv, f_send, f_recv, h_send, h_recv,
):
    me = lax.axis_index("seq")
    fx = lax.axis_index("ffn")
    my_y = me // GRP
    my_zc = me % GRP
    left, right, far = (fx + 3) % 4, (fx + 1) % 4, (fx + 2) % 4

    cols = pl.ds(pl.multiple_of(fx * Q, Q), Q)
    loads = [
        (child.at[:, cols], child_v),
        (parent.at[:, cols], parent_v),
        (wq, wqkv.at[:, pl.ds(0, Q)]),
        (wk, wqkv.at[:, pl.ds(Q, Q)]),
        (wv, wqkv.at[:, pl.ds(2 * Q, Q)]),
        (wo, wo_v),
        (wu, wu_v),
        (wd, wd_v),
    ]
    loads = [pltpu.make_async_copy(s, d, in_sem.at[i]) for i, (s, d) in enumerate(loads)]
    for copy in loads:
        copy.start()

    barrier = pltpu.get_barrier_semaphore()

    def greet(k, _):
        pl.semaphore_signal(
            barrier, inc=1, device_id=((me + k) % N, fx), device_id_type=MESH
        )
        return 0

    lax.fori_loop(1, N, greet, 0)
    for k in (1, 2, 3):
        pl.semaphore_signal(barrier, inc=1, device_id=(me, (fx + k) % 4), device_id_type=MESH)

    owners = own_row[...]
    member = iota((N, TOK), 0) == owners
    matched = member.astype(F32)
    upper = (iota((TOK, TOK), 0) <= iota((TOK, TOK), 1)).astype(F32).astype(BF16)
    counts = nn(matched.astype(BF16), upper)
    within = jnp.sum(matched * (counts - 1.0), axis=0, keepdims=True)
    target = owners.astype(F32) * float(CAP) + within
    eye = (iota((TOK, TOK), 0) == iota((TOK, TOK), 1)).astype(F32)
    target_col = nt(eye, jnp.broadcast_to(target, (8, TOK)), EXACT)[:, 0:1]
    pick_t[...] = (
        (iota((TOK, SLOT), 1) == (target_col + 0.5).astype(jnp.int32)).astype(F32).astype(BF16)
    )
    parents = (iota((PAR, TOK), 0) == cp_row[...]).astype(F32).astype(BF16)
    loads[0].wait()
    loads[1].wait()
    joined[...] = (child_v[...].astype(F32) + tn(parents, parent_v[...])).astype(BF16)
    target_int = (target + 0.5).astype(jnp.int32)
    for i in range(4):
        pick = (iota((CH, TOK), 0) + i * CH == target_int).astype(F32).astype(BF16)
        outgoing[pl.ds(i * GRP, GRP)] = (
            nn(pick, joined[...]).astype(BF16).reshape(GRP, CAP, Q)
        )

    pl.semaphore_wait(barrier, N - 1 + 3)

    def slot_copy(dest, rel):
        return pltpu.make_async_remote_copy(
            src_ref=outgoing.at[dest],
            dst_ref=slots.at[fx, me],
            send_sem=a_send,
            recv_sem=a_recv.at[(4 - rel) % 4],
            device_id=(dest, fx),
            device_id_type=MESH,
        )

    own_slots = pltpu.make_async_copy(outgoing.at[me], slots.at[fx, me], a_recv.at[0])
    own_slots.start()
    for rel in REL:
        base = (my_y + rel) % 4 * GRP

        def send(j, _, base=base, rel=rel):
            half = (j + 1) // 2
            off = half * (j % 2) + (GRP - half) * (1 - j % 2)
            slot_copy(base + (my_zc + off) % GRP, rel).start()
            return 0

        lax.fori_loop(1 if rel == 0 else 0, GRP, send, 0)

    causal = iota((CH, CH), 0) >= iota((CH, CH), 1)
    tri = causal.astype(F32)
    lane_head = iota((1, Q), 1) // HD

    def spread(columns):
        wide = jnp.zeros((columns.shape[0], Q), F32)
        for h in range(HEADS):
            wide = jnp.where(lane_head == h, columns[:, h : h + 1], wide)
        return wide

    block_end = jnp.zeros((1, HEADS), F32)
    for y in range(4):
        g = gate[:, pl.ds(y * CH, CH)]
        crow[y] = nt(g, tri, EXACT)
        columns = nt(tri, g, EXACT)
        ccol[y] = columns
        offs[y] = spread(block_end)
        block_end = block_end + columns[CH - 1 : CH, :]

    def ring(src, dst, send_sem, recv_sem, to):
        return pltpu.make_async_remote_copy(
            src_ref=src, dst_ref=dst, send_sem=send_sem, recv_sem=recv_sem,
            device_id=(me, to), device_id_type=MESH,
        )

    def gather_first(rel):
        rows = pl.ds((my_y + rel) % 4 * GRP, GRP)
        mine = slots.at[fx, rows]
        return [
            ring(mine, mine, g_send.at[rel, 0], g_recv.at[rel, 0], right),
            ring(mine, mine, g_send.at[rel, 1], g_recv.at[rel, 1], left),
        ]

    def gather_second(rel):
        start = (my_y + rel) % 4 * GRP
        a = slots.at[left, pl.ds(start, GRP // 2)]
        b = slots.at[right, pl.ds(start + GRP // 2, GRP // 2)]
        return [
            ring(a, a, g_send.at[rel, 2], g_recv.at[rel, 2], right),
            ring(b, b, g_send.at[rel, 3], g_recv.at[rel, 3], left),
        ]

    def slots_in(rel):
        here = slots.at[fx, pl.ds((my_y + rel) % 4 * GRP, GRP)]
        pltpu.make_async_copy(here, here, a_recv.at[rel]).wait()
        for copy in gather_first(rel):
            copy.start()

    def slots_on(rel):
        for copy, after in zip(gather_first(rel), gather_second(rel)):
            copy.wait_recv()
            after.start()

    def project(rel):
        y = (my_y + rel) % 4
        for copy in gather_second(rel):
            copy.wait_recv()
        squares = jnp.zeros((CH, 1), F32)
        for q in range(4):
            x = slots[q, pl.ds(y * GRP, GRP)].reshape(CH, Q).astype(F32)
            squares = squares + jnp.sum(x * x, axis=1, keepdims=True)
        scale = lax.rsqrt(squares / D + EPS)
        for q in range(4):
            x = slots[q, pl.ds(y * GRP, GRP)].reshape(CH, Q).astype(F32)
            gain = ngain[:, pl.ds(q * Q, Q)].astype(F32)
            normed[:, pl.ds(q * Q, Q)] = (x * scale * gain).astype(BF16)
        qkv[y] = nn(normed[...], wqkv[...]).astype(BF16)

    order = list(REL)
    for i in range(6):
        if i < 4:
            slots_in(order[i])
        if 1 <= i < 5:
            slots_on(order[i - 1])
        if i == 1:
            for copy in loads[2:5]:
                copy.wait()
        if i >= 2:
            project(order[i - 2])

    same_head = iota((Q, Q), 0) // HD == iota((Q, Q), 1) // HD
    carried = jnp.zeros((Q, Q), F32)
    for y in range(4):
        loc[y] = carried
        ends = ccol[y, pl.ds(CH - 1, 1), :]
        fade = jnp.exp(spread(ends - ccol[y]))
        added = tn(
            (qkv[y, :, pl.ds(Q, Q)].astype(F32) * fade).astype(BF16),
            qkv[y, :, pl.ds(2 * Q, Q)],
        )
        carried = jnp.exp(spread(ends)) * carried + jnp.where(same_head, added, 0.0)
    state = jnp.zeros((HD, Q), F32)
    for h in range(HEADS):
        state = state + carried[h * HD : (h + 1) * HD, :]
    lane = iota((1, 128), 1)
    ends = jnp.zeros((1, 128), F32)
    for h in range(HEADS):
        ends = jnp.where(lane == h, block_end[:, h : h + 1], ends)
    s_send[:, 0, :] = jnp.concatenate([state, jnp.broadcast_to(ends, (HD, 128))], axis=1)

    def to_all(src, dst, send_sem, recv_sem):
        pltpu.make_async_copy(src.at[me], dst.at[me], recv_sem).start()

        def send(k, _):
            dest = (me + k) % N
            pltpu.make_async_remote_copy(
                src_ref=src.at[dest], dst_ref=dst.at[me], send_sem=send_sem, recv_sem=recv_sem,
                device_id=(dest, fx), device_id_type=MESH,
            ).start()
            return 0

        lax.fori_loop(1, N, send, 0)

    def arrived(ref, sem):
        pltpu.make_async_copy(ref, ref, sem).wait()

    to_all(s_send, s_recv, st_send, st_recv)

    def inside(y):
        q = qkv[y, :, pl.ds(0, Q)]
        k = qkv[y, :, pl.ds(Q, Q)]
        v = qkv[y, :, pl.ds(2 * Q, Q)]
        total = jnp.zeros((CH, Q), F32)
        for h in range(HEADS):
            mine = (lane_head == h).astype(F32).astype(BF16)
            scores = nt(q * mine, k)
            spacing = ccol[y, :, pl.ds(h, 1)] - crow[y, pl.ds(h, 1), :]
            decay = jnp.where(causal, jnp.exp(jnp.minimum(spacing, 0.0)), 0.0)
            total = total + nn((scores * decay).astype(BF16), v * mine)
        att[y] = total

    inside(0)
    inside(1)
    arrived(s_recv, st_recv)
    got = s_recv[:, 0, :]
    got_ends = got[:, Q:]
    states = got[:, :Q]
    tri_n = (iota((N, N), 0) >= iota((N, N), 1)).astype(F32)
    upto = nn(tri_n, got_ends, EXACT)
    before = upto - got_ends
    upto_t = upto.T
    earlier = iota((N, N), 0) > iota((N, N), 1)
    prefix = jnp.zeros((N, Q), F32)
    for h in range(HEADS):
        spacing = before[:, h : h + 1] - upto_t[h : h + 1, :]
        weight = jnp.where(earlier, jnp.exp(jnp.minimum(spacing, 0.0)), 0.0)
        prefix = jnp.where(lane_head == h, nn(weight, states, EXACT), prefix)
    p_send[:, 0, :] = prefix
    to_all(p_send, p_recv, pf_send, pf_recv)
    inside(2)
    inside(3)
    arrived(p_recv, pf_recv)
    incoming = p_recv[:, 0, :]
    incoming = jnp.where(same_head, jnp.concatenate([incoming] * HEADS, axis=0), 0.0)

    ones_head = same_head.astype(F32).astype(BF16)
    for rel in REL:
        y = (my_y + rel) % 4
        at_start = jnp.exp(offs[y]) * incoming + loc[y]
        outside = nn(qkv[y, :, pl.ds(0, Q)], at_start.astype(BF16))
        o = att[y] + jnp.exp(spread(ccol[y])) * outside
        squares = o * o
        high = squares.astype(BF16)
        low = (squares - high.astype(F32)).astype(BF16)
        mean = (nn(high, ones_head) + nn(low, ones_head)) / HD
        o = o * lax.rsqrt(mean + EPS) * hgain[...].astype(F32)
        heads_out[pl.ds(y * GRP, GRP)] = o.astype(BF16).reshape(GRP, CAP, Q)
        if rel == 0:
            pltpu.make_async_copy(heads_out.at[me], back.at[me], b_recv).start()

        def send(j, _, y=y):
            half = (j + 1) // 2
            off = half * (j % 2) + (GRP - half) * (1 - j % 2)
            dest = y * GRP + (my_zc + off) % GRP
            pltpu.make_async_remote_copy(
                src_ref=heads_out.at[dest], dst_ref=back.at[me], send_sem=b_send, recv_sem=b_recv,
                device_id=(dest, fx), device_id_type=MESH,
            ).start()
            return 0

        lax.fori_loop(1 if rel == 0 else 0, GRP, send, 0)

    top, bottom = pl.ds(0, HALF), pl.ds(HALF, HALF)

    def scatter_first(s, c):
        return [
            ring(part.at[s, c, far, top], via.at[s, c, 0], v_send.at[s, c, 0], v_recv.at[s, c, 0], right),
            ring(part.at[s, c, far, bottom], via.at[s, c, 1], v_send.at[s, c, 1], v_recv.at[s, c, 1], left),
        ]

    def scatter_own(s, c):
        return [
            ring(part.at[s, c, right, bottom], fin.at[s, c, 0, 1], f_send.at[s, c, 0, 1], f_recv.at[s, c, 0, 1], right),
            ring(part.at[s, c, left, top], fin.at[s, c, 1, 0], f_send.at[s, c, 1, 0], f_recv.at[s, c, 1, 0], left),
        ]

    def scatter_joint(s, c):
        return [
            ring(comb.at[s, c, 0], fin.at[s, c, 0, 0], f_send.at[s, c, 0, 0], f_recv.at[s, c, 0, 0], right),
            ring(comb.at[s, c, 1], fin.at[s, c, 1, 1], f_send.at[s, c, 1, 1], f_recv.at[s, c, 1, 1], left),
        ]

    def scatter_start(s, c, product):
        for q in range(4):
            part[s, c, q] = product[:, q * Q : (q + 1) * Q].astype(BF16)
        for copy in scatter_first(s, c) + scatter_own(s, c):
            copy.start()

    def scatter_on(s, c):
        pieces = [(right, top), (left, bottom)]
        for d, (copy, after) in enumerate(zip(scatter_first(s, c), scatter_joint(s, c))):
            copy.wait_recv()
            whose, rows = pieces[d]
            comb[s, c, d] = (
                part[s, c, whose, rows, :].astype(F32) + via[s, c, d].astype(F32)
            ).astype(BF16)
            after.start()

    def scattered(s, c):
        for copy in scatter_own(s, c) + scatter_joint(s, c):
            copy.wait_recv()
        total = part[s, c, fx].astype(F32)
        for d in range(2):
            total = total + fin[s, c, d].reshape(ROWS, Q).astype(F32)
        return total

    def hidden_first(c):
        mine = hb.at[fx, c]
        return [
            ring(mine, mine, h_send.at[c, 0], h_recv.at[c, 0], right),
            ring(mine, mine, h_send.at[c, 1], h_recv.at[c, 1], left),
        ]

    def hidden_second(c):
        a, b = hb.at[left, c, top], hb.at[right, c, bottom]
        return [
            ring(a, a, h_send.at[c, 2], h_recv.at[c, 2], right),
            ring(b, b, h_send.at[c, 3], h_recv.at[c, 3], left),
        ]

    def hidden_start(c):
        rows = pl.ds(c * ROWS, ROWS)
        value = joined[rows, :].astype(F32) + scattered(0, c)
        hid[c] = value
        hb[fx, c] = value.astype(BF16)
        for copy in hidden_first(c):
            copy.start()

    def hidden_on(c):
        for copy, after in zip(hidden_first(c), hidden_second(c)):
            copy.wait_recv()
            after.start()

    def feed_forward(c):
        for copy in hidden_second(c):
            copy.wait_recv()
        squares = jnp.zeros((ROWS, 1), F32)
        scaled = []
        for q in range(4):
            x = hb[q, c].astype(F32)
            squares = squares + jnp.sum(x * x, axis=1, keepdims=True)
            scaled.append((x * fgain[:, pl.ds(q * Q, Q)].astype(F32)).astype(BF16))
        u = nn(jnp.concatenate(scaled, axis=1), wu_v[...]) * lax.rsqrt(squares / D + EPS)
        expanded = jax.nn.gelu(u).astype(BF16)
        scatter_start(1, c, nn(expanded, wd_v[...]))

    def finish(c):
        out[pl.ds(c * ROWS, ROWS), :] = (hid[c] + scattered(1, c)).astype(BF16)

    for copy in loads[5:]:
        copy.wait()
    arrived(back, b_recv)
    for c in range(4):
        rows = pl.ds(c * ROWS, ROWS)
        heads = nn(pick_t[rows, :], back[...].reshape(SLOT, Q)).astype(BF16)
        scatter_start(0, c, nn(heads, wo_v[...]))
    steps = [
        (0, lambda c: scatter_on(0, c)),
        (1, hidden_start),
        (2, hidden_on),
        (3, feed_forward),
        (5, lambda c: scatter_on(1, c)),
        (6, finish),
    ]
    for i in range(10):
        for delay, step in steps:
            if 0 <= i - delay < 4:
                step(i - delay)

    arrived(outgoing.at[pl.ds(0, N - 1)], a_send)
    arrived(s_send.at[pl.ds(0, N - 1)], st_send)
    arrived(p_send.at[pl.ds(0, N - 1)], pf_send)
    arrived(heads_out.at[pl.ds(0, N - 1)], b_send)
    for rel in range(4):
        for copy in gather_first(rel) + gather_second(rel):
            copy.wait_send()
        for copy in hidden_first(rel) + hidden_second(rel):
            copy.wait_send()
        for s in range(2):
            for copy in scatter_first(s, rel) + scatter_own(s, rel) + scatter_joint(s, rel):
                copy.wait_send()


def on_device(
    child_feat, parent_feat, child_parent, owner, log_gate, norm_gain, w_query, w_key, w_value,
    head_gain, w_out, ffn_gain, w_up, w_down,
):
    vmem = pl.BlockSpec(memory_space=pltpu.VMEM)
    anywhere = pl.BlockSpec(memory_space=pl.ANY)
    dma = pltpu.SemaphoreType.DMA
    return pl.pallas_call(
        kernel,
        out_shape=jax.ShapeDtypeStruct((TOK, Q), BF16),
        in_specs=[
            anywhere, anywhere, vmem, vmem, vmem, vmem, anywhere, anywhere, anywhere, vmem,
            anywhere, vmem, anywhere, anywhere,
        ],
        out_specs=vmem,
        scratch_shapes=[
            pltpu.VMEM((TOK, Q), BF16),
            pltpu.VMEM((PAR, Q), BF16),
            pltpu.VMEM((D, 3 * Q), BF16),
            pltpu.VMEM((Q, D), BF16),
            pltpu.VMEM((D, D), BF16),
            pltpu.VMEM((D, D), BF16),
            pltpu.VMEM((TOK, Q), BF16),
            pltpu.VMEM((TOK, SLOT), BF16),
            pltpu.VMEM((N, CAP, Q), BF16),
            pltpu.VMEM((4, N, CAP, Q), BF16),
            pltpu.VMEM((CH, D), BF16),
            pltpu.VMEM((4, CH, 3 * Q), BF16),
            pltpu.VMEM((4, CH, Q), F32),
            pltpu.VMEM((4, CH, HEADS), F32),
            pltpu.VMEM((4, HEADS, CH), F32),
            pltpu.VMEM((4, Q, Q), F32),
            pltpu.VMEM((4, 1, Q), F32),
            pltpu.VMEM((N, 1, Q + 128), F32),
            pltpu.VMEM((N, 1, Q + 128), F32),
            pltpu.VMEM((N, 1, Q), F32),
            pltpu.VMEM((N, 1, Q), F32),
            pltpu.VMEM((N, CAP, Q), BF16),
            pltpu.VMEM((N, CAP, Q), BF16),
            pltpu.VMEM((2, 4, 4, ROWS, Q), BF16),
            pltpu.VMEM((2, 4, 2, HALF, Q), BF16),
            pltpu.VMEM((2, 4, 2, HALF, Q), BF16),
            pltpu.VMEM((2, 4, 2, 2, HALF, Q), BF16),
            pltpu.VMEM((4, ROWS, Q), F32),
            pltpu.VMEM((4, 4, ROWS, Q), BF16),
            dma((8,)),
            dma,
            dma((4,)),
            dma((4, 4)),
            dma((4, 4)),
            dma, dma, dma, dma, dma, dma,
            dma((2, 4, 2)),
            dma((2, 4, 2)),
            dma((2, 4, 2, 2)),
            dma((2, 4, 2, 2)),
            dma((4, 4)),
            dma((4, 4)),
        ],
        compiler_params=pltpu.CompilerParams(
            collective_id=0, has_side_effects=True, vmem_limit_bytes=56 * 1024 * 1024
        ),
        name="block",
    )(
        child_feat,
        parent_feat,
        child_parent.reshape(1, TOK),
        owner.reshape(1, TOK),
        log_gate,
        norm_gain.reshape(1, D),
        w_query,
        w_key,
        w_value,
        head_gain.reshape(1, Q),
        w_out,
        ffn_gain.reshape(1, D),
        w_up,
        w_down,
    )


def solution(mesh):
    seq, ffn = "seq", "ffn"
    in_specs = (
        P(seq, None), P(seq, None), P(seq), P(seq, None), P(ffn, seq), P(), P(None, ffn),
        P(None, ffn), P(None, ffn), P(ffn), P(ffn, None), P(), P(None, ffn), P(ffn, None),
    )
    return jax.shard_map(
        on_device, mesh=mesh, in_specs=in_specs, out_specs=P(seq, ffn), check_vma=False
    )
```

time: 255 us -> 117 us (0.46)
  blocking collectives: 131 us -> 0 us
  Pallas kernels: 0 us -> 111 us
  waiting for transfers between devices: 31.4 us -> 0 us
  starting transfers between devices: 30.2 us -> 0 us
  matrix products: 28.2 us -> 0 us
  other arithmetic: 21 us -> 0 us
  local copies, waits for them, and re-layouts: 9.13 us -> 5.46 us
    pallas_call x0 -> x1, Pallas kernels: none -> 111 us  [on_device(): pl.pallas_call(kernel, out_shape=jax.ShapeDtypeStruct((TOK, Q), BF16), in...]
    all_gather x5 -> x0, blocking collectives: 67.9 us -> none  [carried_in(): lax.all_gather(part.astype(kind), axis)]
    all_to_all x3 -> x0, blocking collectives: 61.1 us -> none  [the longest x2 41.4 us: sum_at_owner(): lax.all_to_all(blocks, axis, split_axis=0, concat_axis=0, tiled=True)]
    all_to_all x4 -> x0, waiting for transfers between devices: 31.4 us -> none  [the longest x1 17.2 us: on_device(): lax.all_to_all(refined.reshape(seq_count, capacity, column_share), SEQ, s...]
    all_to_all x4 -> x0, starting transfers between devices: 30.2 us -> none  [the longest x1 12.1 us: on_device(): lax.all_to_all(outgoing.reshape(seq_count, capacity, column_share), SEQ,...]
    dot_general x9 -> x0, matrix products: 28.2 us -> none  [the longest x1 9.56 us: on_device(): jnp.einsum('hst,thd->shd', mixing, value_rows, preferred_element_type=jnp...]
    convert_element_type x12 -> x0, other arithmetic: 7.25 us -> none  [the longest x1 4.11 us: on_device(): row_norm(residual_in, norm_gain.astype(jnp.float32)).astype(jnp.bfloat16)]
    reduce_sum x6 -> x0, other arithmetic: 5.1 us -> none  [the longest x1 2.07 us: row_norm(): jnp.mean(values * values, axis=-1, keepdims=True) + EPSILON]
  transfers between devices with their start and end apart: 4 -> 0, of which waited for: 3 -> 0; matrix products, arithmetic and copies ran while one was open for 2% -> 0% of each run, Pallas kernels for 0% -> 0%
where the time goes in v1:
time: 117 us
  Pallas kernels  111 us (95%)
  local copies, waits for them, and re-layouts  5.46 us (5%)
    pallas_call x1, Pallas kernels, on_device(): pl.pallas_call(kernel, out_shape=jax.ShapeDtypeStruct((TOK, Q), BF16), in...  111 us

profile of v1, /device:TPU:2, one launch (start us, length us, event | category | flops | bytes accessed | tf_op | source)
XLA Modules:
  0.0 116.6 jit_solution(15081083262013314915)
XLA Ops:
  0.0 1.2 %reshape.18.hgain = bf16[1,256]{1,0:T(2,128)(2,1)} reshape(bf16[256]{0:T(256)(128)(2,1)} %param.23) | data formatting | bytes 1024 | tf_op jit(solution)/shard_map/reshape | solution.py:513
  1.2 1.3 %reshape.17.ngain = bf16[1,1024]{1,0:T(2,128)(2,1)} reshape(bf16[1024]{0:T(1024)(128)(2,1)} %param.19) | data formatting | bytes 4096 | tf_op jit(solution)/shard_map/reshape | solution.py:509
  2.5 1.3 %reshape.19.fgain = bf16[1,1024]{1,0:T(2,128)(2,1)} reshape(bf16[1024]{0:T(1024)(128)(2,1)} %param.25) | data formatting | bytes 4096 | tf_op jit(solution)/shard_map/reshape | solution.py:515
  3.8 111.1 %block.1 = bf16[512,256]{1,0:T(8,128)(2,1)} custom-call(bf16[512,1024]{1,0:T(8,128)(2,1)} %child.1, bf16[64,1024]{1,0:T(8,128)(2,1)} %parent.1, s32[1,512]{1,0:T(1,128)} %bitcast.2, s32[1,512]{1,0:T(1,128)} %bitcast.3, f32[4,1024]{1,0:T(4,128)} %gate.1, bf16[1,1024]{1,0:T(2,128)(2,1)} %reshape.17.ngain, bf16[1024,256]{1,0:T(8,128)(2,1)} %wq.1, ...), custom_call_target="tpu_custom_call" | custom-call | tf_op jit(solution)/shard_map/block/pallas_call | solution.py:448
  114.9 1.7 %copy.16 = bf16[512,256]{1,0:T(8,128)(2,1)} copy(bf16[512,256]{1,0:T(8,128)(2,1)} %block.1) | data formatting | bytes 524288

commit v2 on v1

--- a/solution.py
+++ b/solution.py
@@ -24,6 +24,7 @@
 MESH = pl.DeviceIdType.MESH
 EXACT = lax.Precision.HIGHEST
 REL = (0, 1, 3, 2)
+AHEAD = 2
 
 
 def nt(a, b, precision=None):
@@ -52,7 +53,7 @@
     s_send, s_recv, p_send, p_recv, heads_out, back,
     part, via, comb, fin, hid, hb,
     in_sem, a_send, a_recv, g_send, g_recv, st_send, st_recv, pf_send, pf_recv, b_send, b_recv,
-    v_send, v_recv, f_send, f_recv, h_send, h_recv,
+    v_send, v_recv, f_send, f_recv, h_send, h_recv, w_send, w_recv,
 ):
     me = lax.axis_index("seq")
     fx = lax.axis_index("ffn")
@@ -62,12 +63,12 @@
 
     cols = pl.ds(pl.multiple_of(fx * Q, Q), Q)
     loads = [
-        (child.at[:, cols], child_v),
-        (parent.at[:, cols], parent_v),
+        (child, child_v),
+        (parent, parent_v),
         (wq, wqkv.at[:, pl.ds(0, Q)]),
         (wk, wqkv.at[:, pl.ds(Q, Q)]),
         (wv, wqkv.at[:, pl.ds(2 * Q, Q)]),
-        (wo, wo_v),
+        (wo, wo_v.at[fx]),
         (wu, wu_v),
         (wd, wd_v),
     ]
@@ -107,7 +108,7 @@
     for i in range(4):
         pick = (iota((CH, TOK), 0) + i * CH == target_int).astype(F32).astype(BF16)
         outgoing[pl.ds(i * GRP, GRP)] = (
-            nn(pick, joined[...]).astype(BF16).reshape(GRP, CAP, Q)
+            nn(pick, joined[:, cols]).astype(BF16).reshape(GRP, CAP, Q)
         )
 
     pl.semaphore_wait(barrier, N - 1 + 3)
@@ -124,16 +125,20 @@
 
     own_slots = pltpu.make_async_copy(outgoing.at[me], slots.at[fx, me], a_recv.at[0])
     own_slots.start()
-    for rel in REL:
+
+    def send_group(rel):
         base = (my_y + rel) % 4 * GRP
 
-        def send(j, _, base=base, rel=rel):
+        def send(j, _):
             half = (j + 1) // 2
             off = half * (j % 2) + (GRP - half) * (1 - j % 2)
             slot_copy(base + (my_zc + off) % GRP, rel).start()
             return 0
 
         lax.fori_loop(1 if rel == 0 else 0, GRP, send, 0)
+
+    for rel in REL[:AHEAD]:
+        send_group(rel)
 
     causal = iota((CH, CH), 0) >= iota((CH, CH), 1)
     tri = causal.astype(F32)
@@ -182,6 +187,9 @@
         pltpu.make_async_copy(here, here, a_recv.at[rel]).wait()
         for copy in gather_first(rel):
             copy.start()
+        place = REL.index((4 - rel) % 4) + AHEAD
+        if place < 4:
+            send_group(REL[place])
 
     def slots_on(rel):
         for copy, after in zip(gather_first(rel), gather_second(rel)):
@@ -199,11 +207,11 @@
         scale = lax.rsqrt(squares / D + EPS)
         for q in range(4):
             x = slots[q, pl.ds(y * GRP, GRP)].reshape(CH, Q).astype(F32)
-            gain = ngain[:, pl.ds(q * Q, Q)].astype(F32)
+            gain = ngain[pl.ds(q * Q, Q)].astype(F32).reshape(1, Q)
             normed[:, pl.ds(q * Q, Q)] = (x * scale * gain).astype(BF16)
         qkv[y] = nn(normed[...], wqkv[...]).astype(BF16)
 
-    order = list(REL)
+    order = [(4 - rel) % 4 for rel in REL]
     for i in range(6):
         if i < 4:
             slots_in(order[i])
@@ -214,6 +222,24 @@
                 copy.wait()
         if i >= 2:
             project(order[i - 2])
+
+    def weights_first():
+        mine = wo_v.at[fx]
+        return [
+            ring(mine, mine, w_send.at[0], w_recv.at[0], right),
+            ring(mine, mine, w_send.at[1], w_recv.at[1], left),
+        ]
+
+    def weights_second():
+        a, b = wo_v.at[left, pl.ds(0, Q // 2)], wo_v.at[right, pl.ds(Q // 2, Q // 2)]
+        return [
+            ring(a, a, w_send.at[2], w_recv.at[2], right),
+            ring(b, b, w_send.at[3], w_recv.at[3], left),
+        ]
+
+    loads[5].wait()
+    for copy in weights_first():
+        copy.start()
 
     same_head = iota((Q, Q), 0) // HD == iota((Q, Q), 1) // HD
     carried = jnp.zeros((Q, Q), F32)
@@ -287,6 +313,9 @@
     inside(2)
     inside(3)
     arrived(p_recv, pf_recv)
+    for copy, after in zip(weights_first(), weights_second()):
+        copy.wait_recv()
+        after.start()
     incoming = p_recv[:, 0, :]
     incoming = jnp.where(same_head, jnp.concatenate([incoming] * HEADS, axis=0), 0.0)
 
@@ -300,7 +329,7 @@
         high = squares.astype(BF16)
         low = (squares - high.astype(F32)).astype(BF16)
         mean = (nn(high, ones_head) + nn(low, ones_head)) / HD
-        o = o * lax.rsqrt(mean + EPS) * hgain[...].astype(F32)
+        o = o * lax.rsqrt(mean + EPS) * hgain[...].astype(F32).reshape(1, Q)
         heads_out[pl.ds(y * GRP, GRP)] = o.astype(BF16).reshape(GRP, CAP, Q)
         if rel == 0:
             pltpu.make_async_copy(heads_out.at[me], back.at[me], b_recv).start()
@@ -319,46 +348,46 @@
 
     top, bottom = pl.ds(0, HALF), pl.ds(HALF, HALF)
 
-    def scatter_first(s, c):
-        return [
-            ring(part.at[s, c, far, top], via.at[s, c, 0], v_send.at[s, c, 0], v_recv.at[s, c, 0], right),
-            ring(part.at[s, c, far, bottom], via.at[s, c, 1], v_send.at[s, c, 1], v_recv.at[s, c, 1], left),
-        ]
-
-    def scatter_own(s, c):
-        return [
-            ring(part.at[s, c, right, bottom], fin.at[s, c, 0, 1], f_send.at[s, c, 0, 1], f_recv.at[s, c, 0, 1], right),
-            ring(part.at[s, c, left, top], fin.at[s, c, 1, 0], f_send.at[s, c, 1, 0], f_recv.at[s, c, 1, 0], left),
-        ]
-
-    def scatter_joint(s, c):
-        return [
-            ring(comb.at[s, c, 0], fin.at[s, c, 0, 0], f_send.at[s, c, 0, 0], f_recv.at[s, c, 0, 0], right),
-            ring(comb.at[s, c, 1], fin.at[s, c, 1, 1], f_send.at[s, c, 1, 1], f_recv.at[s, c, 1, 1], left),
-        ]
-
-    def scatter_start(s, c, product):
+    def scatter_first(c):
+        return [
+            ring(part.at[c, far, top], via.at[c, 0], v_send.at[c, 0], v_recv.at[c, 0], right),
+            ring(part.at[c, far, bottom], via.at[c, 1], v_send.at[c, 1], v_recv.at[c, 1], left),
+        ]
+
+    def scatter_own(c):
+        return [
+            ring(part.at[c, right, bottom], fin.at[c, 0, 1], f_send.at[c, 0, 1], f_recv.at[c, 0, 1], right),
+            ring(part.at[c, left, top], fin.at[c, 1, 0], f_send.at[c, 1, 0], f_recv.at[c, 1, 0], left),
+        ]
+
+    def scatter_joint(c):
+        return [
+            ring(comb.at[c, 0], fin.at[c, 0, 0], f_send.at[c, 0, 0], f_recv.at[c, 0, 0], right),
+            ring(comb.at[c, 1], fin.at[c, 1, 1], f_send.at[c, 1, 1], f_recv.at[c, 1, 1], left),
+        ]
+
+    def scatter_start(c, product):
         for q in range(4):
-            part[s, c, q] = product[:, q * Q : (q + 1) * Q].astype(BF16)
-        for copy in scatter_first(s, c) + scatter_own(s, c):
+            part[c, q] = product[:, q * Q : (q + 1) * Q].astype(BF16)
+        for copy in scatter_first(c) + scatter_own(c):
             copy.start()
 
-    def scatter_on(s, c):
+    def scatter_on(c):
         pieces = [(right, top), (left, bottom)]
-        for d, (copy, after) in enumerate(zip(scatter_first(s, c), scatter_joint(s, c))):
+        for d, (copy, after) in enumerate(zip(scatter_first(c), scatter_joint(c))):
             copy.wait_recv()
             whose, rows = pieces[d]
-            comb[s, c, d] = (
-                part[s, c, whose, rows, :].astype(F32) + via[s, c, d].astype(F32)
+            comb[c, d] = (
+                part[c, whose, rows, :].astype(F32) + via[c, d].astype(F32)
             ).astype(BF16)
             after.start()
 
-    def scattered(s, c):
-        for copy in scatter_own(s, c) + scatter_joint(s, c):
+    def scattered(c):
+        for copy in scatter_own(c) + scatter_joint(c):
             copy.wait_recv()
-        total = part[s, c, fx].astype(F32)
+        total = part[c, fx].astype(F32)
         for d in range(2):
-            total = total + fin[s, c, d].reshape(ROWS, Q).astype(F32)
+            total = total + fin[c, d].reshape(ROWS, Q).astype(F32)
         return total
 
     def hidden_first(c):
@@ -374,14 +403,6 @@
             ring(a, a, h_send.at[c, 2], h_recv.at[c, 2], right),
             ring(b, b, h_send.at[c, 3], h_recv.at[c, 3], left),
         ]
-
-    def hidden_start(c):
-        rows = pl.ds(c * ROWS, ROWS)
-        value = joined[rows, :].astype(F32) + scattered(0, c)
-        hid[c] = value
-        hb[fx, c] = value.astype(BF16)
-        for copy in hidden_first(c):
-            copy.start()
 
     def hidden_on(c):
         for copy, after in zip(hidden_first(c), hidden_second(c)):
@@ -389,37 +410,33 @@
             after.start()
 
     def feed_forward(c):
+        rows = pl.ds(c * ROWS, ROWS)
         for copy in hidden_second(c):
             copy.wait_recv()
-        squares = jnp.zeros((ROWS, 1), F32)
-        scaled = []
+        heads = jnp.concatenate([hb[q, c] for q in range(4)], axis=1)
+        hidden = joined[rows, :].astype(F32) + nn(heads, wo_v[...].reshape(D, D))
         for q in range(4):
-            x = hb[q, c].astype(F32)
-            squares = squares + jnp.sum(x * x, axis=1, keepdims=True)
-            scaled.append((x * fgain[:, pl.ds(q * Q, Q)].astype(F32)).astype(BF16))
-        u = nn(jnp.concatenate(scaled, axis=1), wu_v[...]) * lax.rsqrt(squares / D + EPS)
-        expanded = jax.nn.gelu(u).astype(BF16)
-        scatter_start(1, c, nn(expanded, wd_v[...]))
+            hid[c, q] = hidden[:, q * Q : (q + 1) * Q]
+        scale = lax.rsqrt(jnp.sum(hidden * hidden, axis=1, keepdims=True) / D + EPS)
+        second = (hidden * scale * fgain[...].astype(F32).reshape(1, D)).astype(BF16)
+        expanded = jax.nn.gelu(nn(second, wu_v[...])).astype(BF16)
+        scatter_start(c, nn(expanded, wd_v[...]))
 
     def finish(c):
-        out[pl.ds(c * ROWS, ROWS), :] = (hid[c] + scattered(1, c)).astype(BF16)
-
-    for copy in loads[5:]:
-        copy.wait()
+        out[pl.ds(c * ROWS, ROWS), :] = (hid[c, fx] + scattered(c)).astype(BF16)
+
     arrived(back, b_recv)
     for c in range(4):
         rows = pl.ds(c * ROWS, ROWS)
-        heads = nn(pick_t[rows, :], back[...].reshape(SLOT, Q)).astype(BF16)
-        scatter_start(0, c, nn(heads, wo_v[...]))
-    steps = [
-        (0, lambda c: scatter_on(0, c)),
-        (1, hidden_start),
-        (2, hidden_on),
-        (3, feed_forward),
-        (5, lambda c: scatter_on(1, c)),
-        (6, finish),
-    ]
-    for i in range(10):
+        hb[fx, c] = nn(pick_t[rows, :], back[...].reshape(SLOT, Q)).astype(BF16)
+        for copy in hidden_first(c):
+            copy.start()
+    for copy in loads[6:]:
+        copy.wait()
+    for copy in weights_second():
+        copy.wait_recv()
+    steps = [(0, hidden_on), (1, feed_forward), (3, scatter_on), (4, finish)]
+    for i in range(8):
         for delay, step in steps:
             if 0 <= i - delay < 4:
                 step(i - delay)
@@ -433,9 +450,10 @@
             copy.wait_send()
         for copy in hidden_first(rel) + hidden_second(rel):
             copy.wait_send()
-        for s in range(2):
-            for copy in scatter_first(s, rel) + scatter_own(s, rel) + scatter_joint(s, rel):
-                copy.wait_send()
+        for copy in scatter_first(rel) + scatter_own(rel) + scatter_joint(rel):
+            copy.wait_send()
+    for copy in weights_first() + weights_second():
+        copy.wait_send()
 
 
 def on_device(
@@ -454,13 +472,13 @@
         ],
         out_specs=vmem,
         scratch_shapes=[
-            pltpu.VMEM((TOK, Q), BF16),
-            pltpu.VMEM((PAR, Q), BF16),
+            pltpu.VMEM((TOK, D), BF16),
+            pltpu.VMEM((PAR, D), BF16),
             pltpu.VMEM((D, 3 * Q), BF16),
-            pltpu.VMEM((Q, D), BF16),
+            pltpu.VMEM((4, Q, D), BF16),
             pltpu.VMEM((D, D), BF16),
             pltpu.VMEM((D, D), BF16),
-            pltpu.VMEM((TOK, Q), BF16),
+            pltpu.VMEM((TOK, D), BF16),
             pltpu.VMEM((TOK, SLOT), BF16),
             pltpu.VMEM((N, CAP, Q), BF16),
             pltpu.VMEM((4, N, CAP, Q), BF16),
@@ -477,11 +495,11 @@
             pltpu.VMEM((N, 1, Q), F32),
             pltpu.VMEM((N, CAP, Q), BF16),
             pltpu.VMEM((N, CAP, Q), BF16),
-            pltpu.VMEM((2, 4, 4, ROWS, Q), BF16),
-            pltpu.VMEM((2, 4, 2, HALF, Q), BF16),
-            pltpu.VMEM((2, 4, 2, HALF, Q), BF16),
-            pltpu.VMEM((2, 4, 2, 2, HALF, Q), BF16),
-            pltpu.VMEM((4, ROWS, Q), F32),
+            pltpu.VMEM((4, 4, ROWS, Q), BF16),
+            pltpu.VMEM((4, 2, HALF, Q), BF16),
+            pltpu.VMEM((4, 2, HALF, Q), BF16),
+            pltpu.VMEM((4, 2, 2, HALF, Q), BF16),
+            pltpu.VMEM((4, 4, ROWS, Q), F32),
             pltpu.VMEM((4, 4, ROWS, Q), BF16),
             dma((8,)),
             dma,
@@ -489,12 +507,14 @@
             dma((4, 4)),
             dma((4, 4)),
             dma, dma, dma, dma, dma, dma,
-            dma((2, 4, 2)),
-            dma((2, 4, 2)),
-            dma((2, 4, 2, 2)),
-            dma((2, 4, 2, 2)),
+            dma((4, 2)),
+            dma((4, 2)),
+            dma((4, 2, 2)),
+            dma((4, 2, 2)),
             dma((4, 4)),
             dma((4, 4)),
+            dma((4,)),
+            dma((4,)),
         ],
         compiler_params=pltpu.CompilerParams(
             collective_id=0, has_side_effects=True, vmem_limit_bytes=56 * 1024 * 1024
@@ -506,13 +526,13 @@
         child_parent.reshape(1, TOK),
         owner.reshape(1, TOK),
         log_gate,
-        norm_gain.reshape(1, D),
+        norm_gain,
         w_query,
         w_key,
         w_value,
-        head_gain.reshape(1, Q),
+        head_gain,
         w_out,
-        ffn_gain.reshape(1, D),
+        ffn_gain,
         w_up,
         w_down,
     )

time: 117 us -> 103 us (0.88)
  Pallas kernels: 111 us -> 101 us
  local copies, waits for them, and re-layouts: 5.46 us -> 1.67 us
    pallas_call x1, Pallas kernels: 111 us -> 101 us  [on_device(): pl.pallas_call(kernel, out_shape=jax.ShapeDtypeStruct((TOK, Q), BF16), in...]
    reshape x3 -> x0, local copies, waits for them, and re-layouts: 3.79 us -> none  [the longest x1 1.28 us: on_device(): norm_gain.reshape(1, D)]
where the time goes in v2:
time: 103 us
  Pallas kernels  101 us (98%)
  local copies, waits for them, and re-layouts  1.67 us (2%)
    pallas_call x1, Pallas kernels, on_device(): pl.pallas_call(kernel, out_shape=jax.ShapeDtypeStruct((TOK, Q), BF16), in...  101 us

profile of v2, /device:TPU:2, one launch (start us, length us, event | category | flops | bytes accessed | tf_op | source)
XLA Modules:
  0.0 102.7 jit_solution(10603781447469344000)
XLA Ops:
  0.0 101.0 %block.1 = bf16[512,256]{1,0:T(8,128)(2,1)} custom-call(bf16[512,1024]{1,0:T(8,128)(2,1)} %child.1, bf16[64,1024]{1,0:T(8,128)(2,1)} %parent.1, s32[1,512]{1,0:T(1,128)} %bitcast.2, s32[1,512]{1,0:T(1,128)} %bitcast.3, f32[4,1024]{1,0:T(4,128)} %gate.1, bf16[1024]{0:T(1024)(128)(2,1)} %ngain.1, bf16[1024,256]{1,0:T(8,128)(2,1)} %wq.1, bf16[1024,256]{1,0:T(8,128)(2,1)} %wk.1, ...), custom_call_target="tpu_custom_call" | custom-call | tf_op jit(solution)/shard_map/block/pallas_call | solution.py:466
  101.0 1.7 %copy.16 = bf16[512,256]{1,0:T(8,128)(2,1)} copy(bf16[512,256]{1,0:T(8,128)(2,1)} %block.1) | data formatting | bytes 524288

commit v3 on v2

--- a/solution.py
+++ b/solution.py
@@ -16,14 +16,17 @@
 CAP = 16
 GRP = 16
 CH = 256
-ROWS = 128
-HALF = 64
+PARTS = 4
+ROWS = TOK // PARTS
+HALF = ROWS // 2
+GATHER_DIRECT = (0,)
+SCATTER_DIRECT = (PARTS - 1,)
 EPS = 1e-05
 F32 = jnp.float32
 BF16 = jnp.bfloat16
 MESH = pl.DeviceIdType.MESH
 EXACT = lax.Precision.HIGHEST
-REL = (0, 1, 3, 2)
+REL = (2, 1, 3, 0)
 AHEAD = 2
 
 
@@ -41,6 +44,10 @@
     return jnp.dot(a, b, precision=precision, preferred_element_type=F32)
 
 
+def farthest_first(j):
+    return GRP // 2 + (j + 1) // 2 * (2 * (j % 2) - 1)
+
+
 def iota(shape, dim):
     return lax.broadcasted_iota(jnp.int32, shape, dim)
 
@@ -48,12 +55,12 @@
 def kernel(
     child, parent, cp_row, own_row, gate, ngain, wq, wk, wv, hgain, wo, fgain, wu, wd,
     out,
-    child_v, parent_v, wqkv, wo_v, wu_v, wd_v,
+    child_q, parent_q, child_v, parent_v, wqkv, wo_v, wu_v, wd_v,
     joined, pick_t, outgoing, slots, normed, qkv, att, ccol, crow, loc, offs,
-    s_send, s_recv, p_send, p_recv, heads_out, back,
+    s_send, s_recv, p_send, p_recv, t_send, t_recv, heads_out, back,
     part, via, comb, fin, hid, hb,
     in_sem, a_send, a_recv, g_send, g_recv, st_send, st_recv, pf_send, pf_recv, b_send, b_recv,
-    v_send, v_recv, f_send, f_recv, h_send, h_recv, w_send, w_recv,
+    v_send, v_recv, f_send, f_recv, h_send, h_recv, w_send, w_recv, t_sent, t_got,
 ):
     me = lax.axis_index("seq")
     fx = lax.axis_index("ffn")
@@ -63,6 +70,8 @@
 
     cols = pl.ds(pl.multiple_of(fx * Q, Q), Q)
     loads = [
+        (child.at[:, cols], child_q),
+        (parent.at[:, cols], parent_q),
         (child, child_v),
         (parent, parent_v),
         (wq, wqkv.at[:, pl.ds(0, Q)]),
@@ -73,7 +82,7 @@
         (wd, wd_v),
     ]
     loads = [pltpu.make_async_copy(s, d, in_sem.at[i]) for i, (s, d) in enumerate(loads)]
-    for copy in loads:
+    for copy in loads[:2]:
         copy.start()
 
     barrier = pltpu.get_barrier_semaphore()
@@ -89,29 +98,18 @@
         pl.semaphore_signal(barrier, inc=1, device_id=(me, (fx + k) % 4), device_id_type=MESH)
 
     owners = own_row[...]
-    member = iota((N, TOK), 0) == owners
-    matched = member.astype(F32)
+    matched = (iota((N, TOK), 0) == owners).astype(F32)
     upper = (iota((TOK, TOK), 0) <= iota((TOK, TOK), 1)).astype(F32).astype(BF16)
     counts = nn(matched.astype(BF16), upper)
     within = jnp.sum(matched * (counts - 1.0), axis=0, keepdims=True)
     target = owners.astype(F32) * float(CAP) + within
-    eye = (iota((TOK, TOK), 0) == iota((TOK, TOK), 1)).astype(F32)
-    target_col = nt(eye, jnp.broadcast_to(target, (8, TOK)), EXACT)[:, 0:1]
-    pick_t[...] = (
-        (iota((TOK, SLOT), 1) == (target_col + 0.5).astype(jnp.int32)).astype(F32).astype(BF16)
-    )
+    target_int = (target + 0.5).astype(jnp.int32)
     parents = (iota((PAR, TOK), 0) == cp_row[...]).astype(F32).astype(BF16)
     loads[0].wait()
     loads[1].wait()
-    joined[...] = (child_v[...].astype(F32) + tn(parents, parent_v[...])).astype(BF16)
-    target_int = (target + 0.5).astype(jnp.int32)
-    for i in range(4):
-        pick = (iota((CH, TOK), 0) + i * CH == target_int).astype(F32).astype(BF16)
-        outgoing[pl.ds(i * GRP, GRP)] = (
-            nn(pick, joined[:, cols]).astype(BF16).reshape(GRP, CAP, Q)
-        )
-
-    pl.semaphore_wait(barrier, N - 1 + 3)
+    for copy in loads[2:]:
+        copy.start()
+    quarter = (child_q[...].astype(F32) + tn(parents, parent_q[...])).astype(BF16)
 
     def slot_copy(dest, rel):
         return pltpu.make_async_remote_copy(
@@ -123,22 +121,38 @@
             device_id_type=MESH,
         )
 
-    own_slots = pltpu.make_async_copy(outgoing.at[me], slots.at[fx, me], a_recv.at[0])
-    own_slots.start()
+    def place_group(rel):
+        y = (my_y + rel) % 4
+        pick = (iota((CH, TOK), 0) + y * CH == target_int).astype(F32).astype(BF16)
+        outgoing[pl.ds(y * GRP, GRP)] = nn(pick, quarter).astype(BF16).reshape(GRP, CAP, Q)
 
     def send_group(rel):
         base = (my_y + rel) % 4 * GRP
+        if rel == 0:
+            pltpu.make_async_copy(outgoing.at[me], slots.at[fx, me], a_recv.at[0]).start()
 
         def send(j, _):
-            half = (j + 1) // 2
-            off = half * (j % 2) + (GRP - half) * (1 - j % 2)
-            slot_copy(base + (my_zc + off) % GRP, rel).start()
+            slot_copy(base + (my_zc + farthest_first(j)) % GRP, rel).start()
             return 0
 
-        lax.fori_loop(1 if rel == 0 else 0, GRP, send, 0)
-
-    for rel in REL[:AHEAD]:
-        send_group(rel)
+        lax.fori_loop(0, GRP - 1 if rel == 0 else GRP, send, 0)
+
+    place_group(REL[0])
+    pl.semaphore_wait(barrier, N - 1 + 3)
+    send_group(REL[0])
+    for rel in REL[1:]:
+        place_group(rel)
+        if REL.index(rel) < AHEAD:
+            send_group(rel)
+
+    eye = (iota((TOK, TOK), 0) == iota((TOK, TOK), 1)).astype(F32)
+    target_col = nt(eye, jnp.broadcast_to(target, (8, TOK)), EXACT)[:, 0:1]
+    pick_t[...] = (
+        (iota((TOK, SLOT), 1) == (target_col + 0.5).astype(jnp.int32)).astype(F32).astype(BF16)
+    )
+    loads[2].wait()
+    loads[3].wait()
+    joined[...] = (child_v[...].astype(F32) + tn(parents, parent_v[...])).astype(BF16)
 
     causal = iota((CH, CH), 0) >= iota((CH, CH), 1)
     tri = causal.astype(F32)
@@ -218,7 +232,7 @@
         if 1 <= i < 5:
             slots_on(order[i - 1])
         if i == 1:
-            for copy in loads[2:5]:
+            for copy in loads[4:7]:
                 copy.wait()
         if i >= 2:
             project(order[i - 2])
@@ -237,7 +251,7 @@
             ring(b, b, w_send.at[3], w_recv.at[3], left),
         ]
 
-    loads[5].wait()
+    loads[7].wait()
     for copy in weights_first():
         copy.start()
 
@@ -259,25 +273,34 @@
     ends = jnp.zeros((1, 128), F32)
     for h in range(HEADS):
         ends = jnp.where(lane == h, block_end[:, h : h + 1], ends)
-    s_send[:, 0, :] = jnp.concatenate([state, jnp.broadcast_to(ends, (HD, 128))], axis=1)
-
-    def to_all(src, dst, send_sem, recv_sem):
-        pltpu.make_async_copy(src.at[me], dst.at[me], recv_sem).start()
+    message = jnp.concatenate([state, jnp.broadcast_to(ends, (HD, 128))], axis=1)
+    for r in range(4):
+        s_send[:, r, :] = message[r * GRP : (r + 1) * GRP, :]
+
+    def to_row(src, dst, send_sem, recv_sem):
+        pltpu.make_async_copy(src.at[my_zc], dst.at[my_zc], recv_sem).start()
 
         def send(k, _):
-            dest = (me + k) % N
+            peer = (my_zc + farthest_first(k)) % GRP
             pltpu.make_async_remote_copy(
-                src_ref=src.at[dest], dst_ref=dst.at[me], send_sem=send_sem, recv_sem=recv_sem,
-                device_id=(dest, fx), device_id_type=MESH,
+                src_ref=src.at[peer], dst_ref=dst.at[my_zc], send_sem=send_sem, recv_sem=recv_sem,
+                device_id=(my_y * GRP + peer, fx), device_id_type=MESH,
             ).start()
             return 0
 
-        lax.fori_loop(1, N, send, 0)
+        lax.fori_loop(0, GRP - 1, send, 0)
+
+    def totals_to(k):
+        return pltpu.make_async_remote_copy(
+            src_ref=t_send, dst_ref=t_recv.at[my_y],
+            send_sem=t_sent.at[k - 1], recv_sem=t_got.at[k - 1],
+            device_id=((my_y + k) % 4 * GRP + my_zc, fx), device_id_type=MESH,
+        )
 
     def arrived(ref, sem):
         pltpu.make_async_copy(ref, ref, sem).wait()
 
-    to_all(s_send, s_recv, st_send, st_recv)
+    to_row(s_send, s_recv, st_send, st_recv)
 
     def inside(y):
         q = qkv[y, :, pl.ds(0, Q)]
@@ -293,30 +316,51 @@
         att[y] = total
 
     inside(0)
-    inside(1)
     arrived(s_recv, st_recv)
-    got = s_recv[:, 0, :]
-    got_ends = got[:, Q:]
-    states = got[:, :Q]
-    tri_n = (iota((N, N), 0) >= iota((N, N), 1)).astype(F32)
-    upto = nn(tri_n, got_ends, EXACT)
-    before = upto - got_ends
+    rows_got = [s_recv[:, r, :] for r in range(4)]
+    got_ends = rows_got[0][:, Q:]
+    states = jnp.concatenate([row[:, :Q] for row in rows_got], axis=1)
+    tri_row = (iota((GRP, GRP), 0) >= iota((GRP, GRP), 1)).astype(F32)
+    upto = nn(tri_row, got_ends, EXACT)
+    row_end = upto[GRP - 1 :, :]
+    before = jnp.concatenate([upto - got_ends, jnp.broadcast_to(row_end, (8, 128))], axis=0)
     upto_t = upto.T
-    earlier = iota((N, N), 0) > iota((N, N), 1)
-    prefix = jnp.zeros((N, Q), F32)
+    earlier = iota((GRP + 8, GRP), 0) > iota((GRP + 8, GRP), 1)
+    wide_head = iota((1, 4 * Q), 1) // HD % HEADS
+    prefix = jnp.zeros((GRP + 8, 4 * Q), F32)
+    passing = jnp.zeros((GRP, 4 * Q), F32)
     for h in range(HEADS):
         spacing = before[:, h : h + 1] - upto_t[h : h + 1, :]
         weight = jnp.where(earlier, jnp.exp(jnp.minimum(spacing, 0.0)), 0.0)
-        prefix = jnp.where(lane_head == h, nn(weight, states, EXACT), prefix)
-    p_send[:, 0, :] = prefix
-    to_all(p_send, p_recv, pf_send, pf_recv)
+        prefix = jnp.where(wide_head == h, nn(weight, states, EXACT), prefix)
+        passing = jnp.where(wide_head == h, jnp.exp(before[:GRP, h : h + 1]), passing)
+    t_send[...] = jnp.concatenate([prefix[GRP : GRP + 1, :], row_end], axis=1)
+    for k in (2, 1, 3):
+        totals_to(k).start()
+    t_recv[my_y] = t_send[...]
+    inside(1)
+    for k in (1, 2, 3):
+        totals_to(k).wait_recv()
+    row_in = jnp.zeros((1, 4 * Q), F32)
+    for y in range(3):
+        total = t_recv[y]
+        fading = jnp.zeros((1, 4 * Q), F32)
+        for h in range(HEADS):
+            fading = jnp.where(
+                wide_head == h, jnp.exp(total[:, 4 * Q + h : 4 * Q + h + 1]), fading
+            )
+        row_in = jnp.where(y < my_y, fading * row_in + total[:, : 4 * Q], row_in)
+    prefix = prefix[:GRP, :] + passing * row_in
+    for r in range(4):
+        p_send[:, r, :] = prefix[:, r * Q : (r + 1) * Q]
+    to_row(p_send, p_recv, pf_send, pf_recv)
     inside(2)
     inside(3)
     arrived(p_recv, pf_recv)
     for copy, after in zip(weights_first(), weights_second()):
         copy.wait_recv()
         after.start()
-    incoming = p_recv[:, 0, :]
+    incoming = jnp.concatenate([p_recv[:, r, :] for r in range(4)], axis=0)
     incoming = jnp.where(same_head, jnp.concatenate([incoming] * HEADS, axis=0), 0.0)
 
     ones_head = same_head.astype(F32).astype(BF16)
@@ -335,20 +379,23 @@
             pltpu.make_async_copy(heads_out.at[me], back.at[me], b_recv).start()
 
         def send(j, _, y=y):
-            half = (j + 1) // 2
-            off = half * (j % 2) + (GRP - half) * (1 - j % 2)
-            dest = y * GRP + (my_zc + off) % GRP
+            dest = y * GRP + (my_zc + farthest_first(j)) % GRP
             pltpu.make_async_remote_copy(
                 src_ref=heads_out.at[dest], dst_ref=back.at[me], send_sem=b_send, recv_sem=b_recv,
                 device_id=(dest, fx), device_id_type=MESH,
             ).start()
             return 0
 
-        lax.fori_loop(1 if rel == 0 else 0, GRP, send, 0)
+        lax.fori_loop(0, GRP - 1 if rel == 0 else GRP, send, 0)
 
     top, bottom = pl.ds(0, HALF), pl.ds(HALF, HALF)
 
     def scatter_first(c):
+        if c in SCATTER_DIRECT:
+            return [
+                ring(part.at[c, far, top], via.at[c, 0], v_send.at[c, 0], v_recv.at[c, 0], far),
+                ring(part.at[c, far, bottom], via.at[c, 1], v_send.at[c, 1], v_recv.at[c, 1], far),
+            ]
         return [
             ring(part.at[c, far, top], via.at[c, 0], v_send.at[c, 0], v_recv.at[c, 0], right),
             ring(part.at[c, far, bottom], via.at[c, 1], v_send.at[c, 1], v_recv.at[c, 1], left),
@@ -361,6 +408,11 @@
         ]
 
     def scatter_joint(c):
+        if c in SCATTER_DIRECT:
+            return [
+                ring(part.at[c, right, top], fin.at[c, 0, 0], f_send.at[c, 0, 0], f_recv.at[c, 0, 0], right),
+                ring(part.at[c, left, bottom], fin.at[c, 1, 1], f_send.at[c, 1, 1], f_recv.at[c, 1, 1], left),
+            ]
         return [
             ring(comb.at[c, 0], fin.at[c, 0, 0], f_send.at[c, 0, 0], f_recv.at[c, 0, 0], right),
             ring(comb.at[c, 1], fin.at[c, 1, 1], f_send.at[c, 1, 1], f_recv.at[c, 1, 1], left),
@@ -371,8 +423,13 @@
             part[c, q] = product[:, q * Q : (q + 1) * Q].astype(BF16)
         for copy in scatter_first(c) + scatter_own(c):
             copy.start()
+        if c in SCATTER_DIRECT:
+            for copy in scatter_joint(c):
+                copy.start()
 
     def scatter_on(c):
+        if c in SCATTER_DIRECT:
+            return
         pieces = [(right, top), (left, bottom)]
         for d, (copy, after) in enumerate(zip(scatter_first(c), scatter_joint(c))):
             copy.wait_recv()
@@ -386,6 +443,10 @@
         for copy in scatter_own(c) + scatter_joint(c):
             copy.wait_recv()
         total = part[c, fx].astype(F32)
+        if c in SCATTER_DIRECT:
+            for copy in scatter_first(c):
+                copy.wait_recv()
+            total = total + via[c].reshape(ROWS, Q).astype(F32)
         for d in range(2):
             total = total + fin[c, d].reshape(ROWS, Q).astype(F32)
         return total
@@ -398,6 +459,9 @@
         ]
 
     def hidden_second(c):
+        if c in GATHER_DIRECT:
+            mine = hb.at[fx, c]
+            return [ring(mine, mine, h_send.at[c, 2], h_recv.at[c, 2], far)]
         a, b = hb.at[left, c, top], hb.at[right, c, bottom]
         return [
             ring(a, a, h_send.at[c, 2], h_recv.at[c, 2], right),
@@ -405,6 +469,10 @@
         ]
 
     def hidden_on(c):
+        if c in GATHER_DIRECT:
+            for copy in hidden_first(c):
+                copy.wait_recv()
+            return
         for copy, after in zip(hidden_first(c), hidden_second(c)):
             copy.wait_recv()
             after.start()
@@ -426,31 +494,34 @@
         out[pl.ds(c * ROWS, ROWS), :] = (hid[c, fx] + scattered(c)).astype(BF16)
 
     arrived(back, b_recv)
-    for c in range(4):
+    for c in range(PARTS):
         rows = pl.ds(c * ROWS, ROWS)
         hb[fx, c] = nn(pick_t[rows, :], back[...].reshape(SLOT, Q)).astype(BF16)
-        for copy in hidden_first(c):
+        for copy in hidden_first(c) + (hidden_second(c) if c in GATHER_DIRECT else []):
             copy.start()
-    for copy in loads[6:]:
+    for copy in loads[8:]:
         copy.wait()
     for copy in weights_second():
         copy.wait_recv()
     steps = [(0, hidden_on), (1, feed_forward), (3, scatter_on), (4, finish)]
-    for i in range(8):
+    for i in range(PARTS + 4):
         for delay, step in steps:
-            if 0 <= i - delay < 4:
+            if 0 <= i - delay < PARTS:
                 step(i - delay)
 
     arrived(outgoing.at[pl.ds(0, N - 1)], a_send)
-    arrived(s_send.at[pl.ds(0, N - 1)], st_send)
-    arrived(p_send.at[pl.ds(0, N - 1)], pf_send)
+    arrived(s_send.at[pl.ds(0, GRP - 1)], st_send)
+    arrived(p_send.at[pl.ds(0, GRP - 1)], pf_send)
+    for k in (1, 2, 3):
+        totals_to(k).wait_send()
     arrived(heads_out.at[pl.ds(0, N - 1)], b_send)
     for rel in range(4):
         for copy in gather_first(rel) + gather_second(rel):
             copy.wait_send()
-        for copy in hidden_first(rel) + hidden_second(rel):
+    for c in range(PARTS):
+        for copy in hidden_first(c) + hidden_second(c):
             copy.wait_send()
-        for copy in scatter_first(rel) + scatter_own(rel) + scatter_joint(rel):
+        for copy in scatter_first(c) + scatter_own(c) + scatter_joint(c):
             copy.wait_send()
     for copy in weights_first() + weights_second():
         copy.wait_send()
@@ -472,6 +543,8 @@
         ],
         out_specs=vmem,
         scratch_shapes=[
+            pltpu.VMEM((TOK, Q), BF16),
+            pltpu.VMEM((PAR, Q), BF16),
             pltpu.VMEM((TOK, D), BF16),
             pltpu.VMEM((PAR, D), BF16),
             pltpu.VMEM((D, 3 * Q), BF16),
@@ -489,32 +562,36 @@
             pltpu.VMEM((4, HEADS, CH), F32),
             pltpu.VMEM((4, Q, Q), F32),
             pltpu.VMEM((4, 1, Q), F32),
-            pltpu.VMEM((N, 1, Q + 128), F32),
-            pltpu.VMEM((N, 1, Q + 128), F32),
-            pltpu.VMEM((N, 1, Q), F32),
-            pltpu.VMEM((N, 1, Q), F32),
+            pltpu.VMEM((GRP, 4, Q + 128), F32),
+            pltpu.VMEM((GRP, 4, Q + 128), F32),
+            pltpu.VMEM((GRP, 4, Q), F32),
+            pltpu.VMEM((GRP, 4, Q), F32),
+            pltpu.VMEM((1, 4 * Q + 128), F32),
+            pltpu.VMEM((4, 1, 4 * Q + 128), F32),
             pltpu.VMEM((N, CAP, Q), BF16),
             pltpu.VMEM((N, CAP, Q), BF16),
-            pltpu.VMEM((4, 4, ROWS, Q), BF16),
-            pltpu.VMEM((4, 2, HALF, Q), BF16),
-            pltpu.VMEM((4, 2, HALF, Q), BF16),
-            pltpu.VMEM((4, 2, 2, HALF, Q), BF16),
-            pltpu.VMEM((4, 4, ROWS, Q), F32),
-            pltpu.VMEM((4, 4, ROWS, Q), BF16),
-            dma((8,)),
+            pltpu.VMEM((PARTS, 4, ROWS, Q), BF16),
+            pltpu.VMEM((PARTS, 2, HALF, Q), BF16),
+            pltpu.VMEM((PARTS, 2, HALF, Q), BF16),
+            pltpu.VMEM((PARTS, 2, 2, HALF, Q), BF16),
+            pltpu.VMEM((PARTS, 4, ROWS, Q), F32),
+            pltpu.VMEM((4, PARTS, ROWS, Q), BF16),
+            dma((10,)),
             dma,
             dma((4,)),
             dma((4, 4)),
             dma((4, 4)),
             dma, dma, dma, dma, dma, dma,
-            dma((4, 2)),
-            dma((4, 2)),
-            dma((4, 2, 2)),
-            dma((4, 2, 2)),
-            dma((4, 4)),
-            dma((4, 4)),
+            dma((PARTS, 2)),
+            dma((PARTS, 2)),
+            dma((PARTS, 2, 2)),
+            dma((PARTS, 2, 2)),
+            dma((PARTS, 4)),
+            dma((PARTS, 4)),
             dma((4,)),
             dma((4,)),
+            dma((3,)),
+            dma((3,)),
         ],
         compiler_params=pltpu.CompilerParams(
             collective_id=0, has_side_effects=True, vmem_limit_bytes=56 * 1024 * 1024

time: 103 us -> 97.6 us (0.948)
  Pallas kernels: 101 us -> 95.5 us
    pallas_call x1, Pallas kernels: 101 us -> 95.5 us  [on_device(): pl.pallas_call(kernel, out_shape=jax.ShapeDtypeStruct((TOK, Q), BF16), in...]
where the time goes in v3:
time: 97.6 us; the launch traced here: 97.2 us
  Pallas kernels  95.5 us (98%)
  local copies, waits for them, and re-layouts  1.67 us (2%)
    pallas_call x1, Pallas kernels, on_device(): pl.pallas_call(kernel, out_shape=jax.ShapeDtypeStruct((TOK, Q), BF16), in...  95.5 us

profile of v3, /device:TPU:2, one launch (start us, length us, event | category | flops | bytes accessed | tf_op | source)
XLA Modules:
  0.0 97.2 jit_solution(3192469741175844514)
XLA Ops:
  0.0 95.5 %block.1 = bf16[512,256]{1,0:T(8,128)(2,1)} custom-call(bf16[512,1024]{1,0:T(8,128)(2,1)} %child.1, bf16[64,1024]{1,0:T(8,128)(2,1)} %parent.1, s32[1,512]{1,0:T(1,128)} %bitcast.2, s32[1,512]{1,0:T(1,128)} %bitcast.3, f32[4,1024]{1,0:T(4,128)} %gate.1, bf16[1024]{0:T(1024)(128)(2,1)} %ngain.1, bf16[1024,256]{1,0:T(8,128)(2,1)} %wq.1, bf16[1024,256]{1,0:T(8,128)(2,1)} %wk.1, ...), custom_call_target="tpu_custom_call" | custom-call | tf_op jit(solution)/shard_map/block/pallas_call | solution.py:537
  95.5 1.7 %copy.16 = bf16[512,256]{1,0:T(8,128)(2,1)} copy(bf16[512,256]{1,0:T(8,128)(2,1)} %block.1) | data formatting | bytes 524288

commit v4 on v3

--- a/solution.py
+++ b/solution.py
@@ -503,7 +503,7 @@
         copy.wait()
     for copy in weights_second():
         copy.wait_recv()
-    steps = [(0, hidden_on), (1, feed_forward), (3, scatter_on), (4, finish)]
+    steps = [(0, hidden_on), (1, feed_forward), (2, scatter_on), (3, finish)]
     for i in range(PARTS + 4):
         for delay, step in steps:
             if 0 <= i - delay < PARTS:

time: 97.6 us -> 97.9 us (level)
  no operation moved by 1% of the time
where the time goes in v4:
time: 97.9 us; the launch traced here: 97.4 us
  Pallas kernels  95.8 us (98%)
  local copies, waits for them, and re-layouts  1.67 us (2%)
    pallas_call x1, Pallas kernels, on_device(): pl.pallas_call(kernel, out_shape=jax.ShapeDtypeStruct((TOK, Q), BF16), in...  95.8 us

profile of v4, /device:TPU:2, one launch (start us, length us, event | category | flops | bytes accessed | tf_op | source)
XLA Modules:
  0.0 97.4 jit_solution(4717302298712044744)
XLA Ops:
  0.0 95.8 %block.1 = bf16[512,256]{1,0:T(8,128)(2,1)} custom-call(bf16[512,1024]{1,0:T(8,128)(2,1)} %child.1, bf16[64,1024]{1,0:T(8,128)(2,1)} %parent.1, s32[1,512]{1,0:T(1,128)} %bitcast.2, s32[1,512]{1,0:T(1,128)} %bitcast.3, f32[4,1024]{1,0:T(4,128)} %gate.1, bf16[1024]{0:T(1024)(128)(2,1)} %ngain.1, bf16[1024,256]{1,0:T(8,128)(2,1)} %wq.1, bf16[1024,256]{1,0:T(8,128)(2,1)} %wk.1, ...), custom_call_target="tpu_custom_call" | custom-call | tf_op jit(solution)/shard_map/block/pallas_call | solution.py:537
  95.8 1.7 %copy.16 = bf16[512,256]{1,0:T(8,128)(2,1)} copy(bf16[512,256]{1,0:T(8,128)(2,1)} %block.1) | data formatting | bytes 524288
